TPU v7x, 32 devices: a whole 2x2x4 slice. The times are simulated.
32 devices in a mesh: srv: 8 (over y, x, core), head: 4 (over z).
Axes of the slice: x: 2, y: 2, z: 4, core: 2. Of those that a mesh axis runs over, the one named last changes fastest.
Arguments:
- queries: bfloat16 [2048, 8192], P('srv', 'head'), may hold values from -200 to 200
- key_value_pair: bfloat16 [2, 2048, 1024], P(None, 'srv', 'head'), may hold values from -200 to 200
- lengths: int32 [8], replicated, may hold values from 1 to 1024, 2048 in all
Outputs:
- attended: bfloat16 [2048, 8192], P(('srv', 'head'))
All inputs are finite; a program needn't handle non-finite values.
Results may differ from a plain program's by a relative error of at most 0.012.
Values may be sent and summed in bfloat16 or wider, within the bound.
A program may use at most 64 MiB of HBM per device.

v0:
```python
import math
import jax
import jax.numpy as jnp
from jax import lax
from jax.sharding import PartitionSpec as P

HEAD_SIZE = 128


def doc_start(doc_lengths, row_ids):
    doc_ends = jnp.cumsum(doc_lengths)
    passed = doc_ends[None, :] <= row_ids[:, None]
    return jnp.max(jnp.where(passed, doc_ends[None, :], 0), axis=1)


def apply_rotary(vectors, positions):
    half_width = vectors.shape[-1] // 2
    steps_up = jnp.arange(half_width, dtype=jnp.float32) * (2.0 / vectors.shape[-1])
    inverse = jnp.exp(-steps_up * math.log(500000.0))
    angles = positions[:, None] * inverse[None, :]
    cosine = jnp.cos(angles)[:, None, :]
    sine_table = jnp.sin(angles)[:, None, :]
    low_half = vectors[..., :half_width]
    high_half = vectors[..., half_width:]
    return jnp.concatenate(
        [low_half * cosine - high_half * sine_table, high_half * cosine + low_half * sine_table],
        axis=-1,
    )


def merge_shard(state, query_group, row_group, start_group, key_rows, value_rows, key_ids):
    run_max, run_total, run_acc = state
    group_rows, kv_local, per_kv, head_width = query_group.shape
    all_heads = kv_local * per_kv
    scores = jnp.einsum(
        "rhgd,khd->hgrk", query_group, key_rows, preferred_element_type=jnp.float32
    ) * HEAD_SIZE ** (-0.5)
    allowed = (
        (key_ids[None, :] <= row_group[:, None]) & (key_ids[None, :] >= start_group[:, None])
    )[None, None]
    masked = jnp.where(allowed, scores, -1e30)
    shard_max = jnp.max(masked, axis=3)
    weights = jnp.where(allowed, jnp.exp(masked - shard_max[..., None]), 0.0)
    shard_total = jnp.sum(weights, axis=3)
    part_value = jnp.einsum(
        "hgrk,khd->rhgd",
        weights.astype(jnp.bfloat16),
        value_rows,
        preferred_element_type=jnp.float32,
    ).reshape(group_rows, all_heads, head_width)
    shard_max = jnp.transpose(shard_max, (2, 0, 1)).reshape(group_rows, all_heads)
    shard_total = jnp.transpose(shard_total, (2, 0, 1)).reshape(group_rows, all_heads)
    new_max = jnp.maximum(run_max, shard_max)
    old_factor = jnp.exp(run_max - new_max)
    new_factor = jnp.exp(shard_max - new_max)
    new_total = run_total * old_factor + shard_total * new_factor
    new_acc = run_acc * old_factor[..., None] + part_value * new_factor[..., None]
    return (new_max, new_total, new_acc)


def attend(query_flat, row_ids, starts, packed_pair, shard_rows, kv_local):
    total_rows, query_width = query_flat.shape
    all_heads = query_width // HEAD_SIZE
    per_kv = all_heads // kv_local
    group_rows = min(total_rows, 64)
    group_count = total_rows // group_rows
    query_view = query_flat.reshape(total_rows, kv_local, per_kv, HEAD_SIZE)

    def add_shard(state, kv_shard, key_low):
        kv_view = kv_shard.reshape(shard_rows, 2, kv_local, HEAD_SIZE)
        key_rows = kv_view[:, 0]
        value_rows = kv_view[:, 1]
        key_ids = key_low + jnp.arange(shard_rows, dtype=jnp.int32)
        key_high = key_low + shard_rows - 1
        updated = []
        for group_index in range(group_count):
            row_slice = slice(group_index * group_rows, (group_index + 1) * group_rows)
            group_state = (state[0][row_slice], state[1][row_slice], state[2][row_slice])
            needed = jnp.any((starts[row_slice] <= key_high) & (row_ids[row_slice] >= key_low))
            group_state = lax.cond(
                needed,
                lambda current, row_slice=row_slice: merge_shard(
                    current,
                    query_view[row_slice],
                    row_ids[row_slice],
                    starts[row_slice],
                    key_rows,
                    value_rows,
                    key_ids,
                ),
                lambda current: current,
                group_state,
            )
            updated.append(group_state)
        return (
            jnp.concatenate([item[0] for item in updated], axis=0),
            jnp.concatenate([item[1] for item in updated], axis=0),
            jnp.concatenate([item[2] for item in updated], axis=0),
        )

    initial = (
        jnp.full((total_rows, all_heads), -1e30, jnp.float32),
        jnp.zeros((total_rows, all_heads), jnp.float32),
        jnp.zeros((total_rows, all_heads, HEAD_SIZE), jnp.float32),
    )
    running = initial
    kv_piece = lax.all_gather(packed_pair, "srv", axis=0, tiled=True)
    shard_count = kv_piece.shape[0] // shard_rows
    shards = kv_piece.reshape(shard_count, shard_rows, kv_piece.shape[1])

    def one_step(current, packed):
        kv_shard, shard_index = packed
        return (add_shard(current, kv_shard, shard_index * shard_rows), None)

    running, _ = lax.scan(one_step, running, (shards, jnp.arange(shard_count, dtype=jnp.int32)))
    run_max, run_total, run_acc = running
    return (run_acc / run_total[..., None]).reshape(total_rows, query_width).astype(jnp.bfloat16)


def body(queries, key_value_pair, lengths):
    tok_rows = queries.shape[0]
    query_width = queries.shape[1]
    all_heads = query_width // HEAD_SIZE
    kv_local = key_value_pair.shape[2] // HEAD_SIZE
    own_index = lax.axis_index("srv")
    local_ids = jnp.arange(tok_rows, dtype=jnp.int32)
    row_ids = own_index * tok_rows + local_ids
    starts = doc_start(lengths, row_ids)
    positions = (row_ids - starts).astype(jnp.float32)
    query_rotated = apply_rotary(
        queries.reshape(tok_rows, all_heads, HEAD_SIZE).astype(jnp.float32), positions
    ).astype(jnp.bfloat16)
    key_rotated = apply_rotary(
        key_value_pair[0].reshape(tok_rows, kv_local, HEAD_SIZE).astype(jnp.float32), positions
    ).astype(jnp.bfloat16)
    packed_pair = jnp.stack(
        [key_rotated, key_value_pair[1].reshape(tok_rows, kv_local, HEAD_SIZE)], axis=1
    )
    packed_pair = packed_pair.reshape(tok_rows, 2 * kv_local * HEAD_SIZE)
    query_flat = query_rotated.reshape(tok_rows, query_width)
    result = attend(query_flat, row_ids, starts, packed_pair, tok_rows, kv_local)
    return lax.all_to_all(result, "head", split_axis=0, concat_axis=1, tiled=True)


def solution(mesh):
    in_specs = (P("srv", "head"), P(None, "srv", "head"), P())
    out_specs = P(("srv", "head"), None)
    return jax.shard_map(body, mesh=mesh, in_specs=in_specs, out_specs=out_specs, check_vma=False)
```

profile of v0, /device:TPU:6, one launch (start us, length us, event | category | flops | bytes accessed | tf_op | source)
XLA Modules:
  0.0 184.0 jit_solution(17758708910333524287)
XLA Ops:
  13.4 25.0 %all-gather.2.cloned.1.call-done = bf16[2048,512]{0,1:T(8,128)(2,1)} async-done(((bf16[256,512]{0,1:T(8,128)(2,1)}), bf16[2048,512]{0,1:T(8,128)(2,1)}) %all-gather.2.cloned.1.call-update) | async-done | bytes 2097168 | tf_op jit(solution)/shard_map/all_gather | solution.py:107
  38.4 3.9 %copy.46 = bf16[2048,512]{1,0:T(8,128)(2,1)} copy(bf16[2048,512]{0,1:T(8,128)(2,1)} %all-gather.2.cloned.1.call-done) | data formatting | bytes 4194304 | tf_op jit(solution)/shard_map/all_gather | solution.py:107
  43.9 108.8 %while.18 = (s32[]{:T(128)}, f32[256,16]{0,1:T(8,128)S(1)}, f32[256,16]{0,1:T(8,128)S(1)}, f32[256,16,128]{2,0,1:T(8,128)}, s32[256]{0:T(256)S(1)}, /*index=5*/s...) while((s32[]{:T(128)}, f32[256,16]{0,1:T(8,128)S(1)}, ...), condition=%wide.region_23.24_spmd, body=%wide.region_2.23_spmd.sunk | while | flops 549692672 | bytes 33666752 | solution.py:115
  46.4 1.7 fusion.81
  55.3 1.7 fusion.81
  64.2 1.7 fusion.81
  67.3 1.8 conditional.11
  69.6 1.9 %conditional.10 = ((f32[64,16]{0,1:T(8,128)S(1)}, f32[64,16]{0,1:T(8,128)S(1)}, f32[64,16,128]{2,0,1:T(8,128)S(1)})) conditional(s32[]{:T(128)} %convert_element_type.111, (f32[64,16]{0,1:T(8,128)S(1)}, f32[64,16]{0,1:T(8,128)S(1)}, f32[64,16,128]{2,0,1:T(8,128)S(1)}) %tuple.134, (s32[256]{0:T(256)S(1)}, s32[256]{0:T(256)S(1)}, s32[256]{0:T(256)S(1)}, ...), branch_computations={%region_9.9_spmd, %region_10.12_spmd} | conditional | flops 137023488 | bytes 5892640 | solution.py:80
  72.2 1.8 conditional.9
  74.6 1.9 %conditional.8 = ((f32[64,16]{0,1:T(8,128)S(1)}, f32[64,16]{0,1:T(8,128)S(1)}, f32[64,16,128]{2,0,1:T(8,128)S(1)})) conditional(s32[]{:T(128)} %convert_element_type.109, (f32[64,16]{0,1:T(8,128)S(1)}, f32[64,16]{0,1:T(8,128)S(1)}, f32[64,16,128]{2,0,1:T(8,128)S(1)}) %tuple.130, (s32[256]{0:T(256)S(1)}, s32[256]{0:T(256)S(1)}, s32[256]{0:T(256)S(1)}, ...), branch_computations={%region_19.19_spmd, %region_20.22_spmd} | conditional | flops 137023488 | bytes 5892640 | solution.py:80
  80.6 1.7 fusion.81
  83.7 1.8 conditional.11
  86.0 1.9 %conditional.10 = ((f32[64,16]{0,1:T(8,128)S(1)}, f32[64,16]{0,1:T(8,128)S(1)}, f32[64,16,128]{2,0,1:T(8,128)S(1)})) conditional(s32[]{:T(128)} %convert_element_type.111, (f32[64,16]{0,1:T(8,128)S(1)}, f32[64,16]{0,1:T(8,128)S(1)}, f32[64,16,128]{2,0,1:T(8,128)S(1)}) %tuple.134, (s32[256]{0:T(256)S(1)}, s32[256]{0:T(256)S(1)}, s32[256]{0:T(256)S(1)}, ...), branch_computations={%region_9.9_spmd, %region_10.12_spmd} | conditional | flops 137023488 | bytes 5892640 | solution.py:80
  88.6 1.8 conditional.9
  91.0 1.9 %conditional.8 = ((f32[64,16]{0,1:T(8,128)S(1)}, f32[64,16]{0,1:T(8,128)S(1)}, f32[64,16,128]{2,0,1:T(8,128)S(1)})) conditional(s32[]{:T(128)} %convert_element_type.109, (f32[64,16]{0,1:T(8,128)S(1)}, f32[64,16]{0,1:T(8,128)S(1)}, f32[64,16,128]{2,0,1:T(8,128)S(1)}) %tuple.130, (s32[256]{0:T(256)S(1)}, s32[256]{0:T(256)S(1)}, s32[256]{0:T(256)S(1)}, ...), branch_computations={%region_19.19_spmd, %region_20.22_spmd} | conditional | flops 137023488 | bytes 5892640 | solution.py:80
  97.0 1.7 fusion.81
  100.1 1.8 conditional.11
  102.4 1.9 %conditional.10 = ((f32[64,16]{0,1:T(8,128)S(1)}, f32[64,16]{0,1:T(8,128)S(1)}, f32[64,16,128]{2,0,1:T(8,128)S(1)})) conditional(s32[]{:T(128)} %convert_element_type.111, (f32[64,16]{0,1:T(8,128)S(1)}, f32[64,16]{0,1:T(8,128)S(1)}, f32[64,16,128]{2,0,1:T(8,128)S(1)}) %tuple.134, (s32[256]{0:T(256)S(1)}, s32[256]{0:T(256)S(1)}, s32[256]{0:T(256)S(1)}, ...), branch_computations={%region_9.9_spmd, %region_10.12_spmd} | conditional | flops 137023488 | bytes 5892640 | solution.py:80
  105.0 1.8 conditional.9
  107.4 1.9 %conditional.8 = ((f32[64,16]{0,1:T(8,128)S(1)}, f32[64,16]{0,1:T(8,128)S(1)}, f32[64,16,128]{2,0,1:T(8,128)S(1)})) conditional(s32[]{:T(128)} %convert_element_type.109, (f32[64,16]{0,1:T(8,128)S(1)}, f32[64,16]{0,1:T(8,128)S(1)}, f32[64,16,128]{2,0,1:T(8,128)S(1)}) %tuple.130, (s32[256]{0:T(256)S(1)}, s32[256]{0:T(256)S(1)}, s32[256]{0:T(256)S(1)}, ...), branch_computations={%region_19.19_spmd, %region_20.22_spmd} | conditional | flops 137023488 | bytes 5892640 | solution.py:80
  113.4 1.7 fusion.81
  116.5 1.8 conditional.11
  118.8 1.9 %conditional.10 = ((f32[64,16]{0,1:T(8,128)S(1)}, f32[64,16]{0,1:T(8,128)S(1)}, f32[64,16,128]{2,0,1:T(8,128)S(1)})) conditional(s32[]{:T(128)} %convert_element_type.111, (f32[64,16]{0,1:T(8,128)S(1)}, f32[64,16]{0,1:T(8,128)S(1)}, f32[64,16,128]{2,0,1:T(8,128)S(1)}) %tuple.134, (s32[256]{0:T(256)S(1)}, s32[256]{0:T(256)S(1)}, s32[256]{0:T(256)S(1)}, ...), branch_computations={%region_9.9_spmd, %region_10.12_spmd} | conditional | flops 137023488 | bytes 5892640 | solution.py:80
  121.4 1.8 conditional.9
  123.8 1.9 %conditional.8 = ((f32[64,16]{0,1:T(8,128)S(1)}, f32[64,16]{0,1:T(8,128)S(1)}, f32[64,16,128]{2,0,1:T(8,128)S(1)})) conditional(s32[]{:T(128)} %convert_element_type.109, (f32[64,16]{0,1:T(8,128)S(1)}, f32[64,16]{0,1:T(8,128)S(1)}, f32[64,16,128]{2,0,1:T(8,128)S(1)}) %tuple.130, (s32[256]{0:T(256)S(1)}, s32[256]{0:T(256)S(1)}, s32[256]{0:T(256)S(1)}, ...), branch_computations={%region_19.19_spmd, %region_20.22_spmd} | conditional | flops 137023488 | bytes 5892640 | solution.py:80
  129.8 1.7 fusion.81
  132.9 1.8 conditional.11
  135.2 1.9 %conditional.10 = ((f32[64,16]{0,1:T(8,128)S(1)}, f32[64,16]{0,1:T(8,128)S(1)}, f32[64,16,128]{2,0,1:T(8,128)S(1)})) conditional(s32[]{:T(128)} %convert_element_type.111, (f32[64,16]{0,1:T(8,128)S(1)}, f32[64,16]{0,1:T(8,128)S(1)}, f32[64,16,128]{2,0,1:T(8,128)S(1)}) %tuple.134, (s32[256]{0:T(256)S(1)}, s32[256]{0:T(256)S(1)}, s32[256]{0:T(256)S(1)}, ...), branch_computations={%region_9.9_spmd, %region_10.12_spmd} | conditional | flops 137023488 | bytes 5892640 | solution.py:80
  137.8 1.8 conditional.9
  140.2 1.9 %conditional.8 = ((f32[64,16]{0,1:T(8,128)S(1)}, f32[64,16]{0,1:T(8,128)S(1)}, f32[64,16,128]{2,0,1:T(8,128)S(1)})) conditional(s32[]{:T(128)} %convert_element_type.109, (f32[64,16]{0,1:T(8,128)S(1)}, f32[64,16]{0,1:T(8,128)S(1)}, f32[64,16,128]{2,0,1:T(8,128)S(1)}) %tuple.130, (s32[256]{0:T(256)S(1)}, s32[256]{0:T(256)S(1)}, s32[256]{0:T(256)S(1)}, ...), branch_computations={%region_19.19_spmd, %region_20.22_spmd} | conditional | flops 137023488 | bytes 5892640 | solution.py:80
  152.7 1.9 %divide_convert_fusion = bf16[256,16,128]{2,0,1:T(8,128)(2,1)S(1)} fusion(f32[256,16,128]{2,0,1:T(8,128)} %get-tuple-element.329, f32[256,16]{0,1:T(8,128)S(1)} %get-tuple-element.330), kind=kLoop, calls=%fused_computation.104 | loop fusion | flops 1048576 | bytes 3162112 | tf_op jit(solution)/shard_map/convert_element_type | solution.py:117
  155.8 20.3 %all_to_all.16 = bf16[4,64,2048]{2,1,0:T(8,128)(2,1)S(1)} all-to-all(bf16[4,64,2048]{2,1,0:T(8,128)(2,1)S(1)} %convert_element_type.90), channel_id=1, replica_groups=mesh['srv'=8,'head'=4] {'head'}, dimensions={0} | all-to-all | bytes 2097152 | tf_op jit(solution)/shard_map/all_to_all | solution.py:142
  (282 shorter events, 81.6 us)
Async XLA Ops:
  6.5 3.6 %copy-start = (bf16[256,2048]{1,0:T(8,128)(2,1)S(1)}, bf16[256,2048]{1,0:T(8,128)(2,1)}, u32[]{:S(2)}) copy-start(bf16[256,2048]{1,0:T(8,128)(2,1)} %param.13) | copy-start | bytes 3145732
  6.5 31.9 %all-gather.2.cloned.1.call-start = ((), (), s32[]{:S(2)}) async-start(), calls=%async_computation.1 | async-start | bytes 2359296 | tf_op jit(solution)/shard_map/all_gather | solution.py:107
Sparse Core Ops, SparseCore 0:
  10.0 28.3 all-gather.1
where the time goes:
time: 185 us; the launch traced here: 184 us
  other arithmetic  46.3 us (25%)
  local copies, waits for them, and re-layouts  38.3 us (21%)
  loops' own time  26.1 us (14%)
  waiting for transfers between devices  25 us (14%)
  blocking collectives  20.3 us (11%)
  matrix products  14.5 us (8%)
  between operations  13.5 us (7%)
    all_gather x1, waiting for transfers between devices, attend(): kv_piece = lax.all_gather(packed_pair, 'srv', axis=0, tiled=True)  25 us
    another operation x1, loops' own time, attend(): lax.scan(one_step, running, (shards, jnp.arange(shard_count, dtype=jnp.in...  24.9 us
    all_to_all x1, blocking collectives, body(): lax.all_to_all(result, 'head', split_axis=0, concat_axis=1, tiled=True)  20.3 us
    dynamic_slice x24, local copies, waits for them, and re-layouts, attend(): lax.scan(one_step, running, (shards, jnp.arange(shard_count, dtype=jnp.in...  13.5 us
    slice x8, local copies, waits for them, and re-layouts, add_shard(): state[2][row_slice]  13.3 us
    concatenate x8, other arithmetic, add_shard(): jnp.concatenate([item[2] for item in updated], axis=0)  11.5 us
    add x20, other arithmetic, merge_shard(): run_acc * old_factor[..., None] + part_value * new_factor[..., None]  10.1 us
    reduce_sum x20, other arithmetic, merge_shard(): shard_total = jnp.sum(weights, axis=3)  8.24 us
  transfers between devices with their start and end apart: 1, of which 1 were waited for; matrix products, arithmetic and copies ran while one was open for 2% of the time, Pallas kernels for 0%

commit v1 on v0

--- a/solution.py
+++ b/solution.py
@@ -5,6 +5,12 @@
 from jax.sharding import PartitionSpec as P
 
 HEAD_SIZE = 128
+
+
+def trade_parts(shard, mesh_axis, split, join):
+    pieces = jnp.split(shard, lax.axis_size(mesh_axis), axis=split)
+    received = lax.all_to_all(jnp.stack(pieces), mesh_axis, 0, 0)
+    return jnp.concatenate(received, axis=join)
 
 
 def doc_start(doc_lengths, row_ids):
@@ -139,7 +145,7 @@
     packed_pair = packed_pair.reshape(tok_rows, 2 * kv_local * HEAD_SIZE)
     query_flat = query_rotated.reshape(tok_rows, query_width)
     result = attend(query_flat, row_ids, starts, packed_pair, tok_rows, kv_local)
-    return lax.all_to_all(result, "head", split_axis=0, concat_axis=1, tiled=True)
+    return trade_parts(result, "head", 0, 1)
 
 
 def solution(mesh):

time: 185 us -> 187 us (1.011)
  no operation moved by 1% of the time
where the time goes in v1:
time: 187 us; the launch traced here: 186 us
  other arithmetic  46.7 us (25%)
  local copies, waits for them, and re-layouts  39.2 us (21%)
  loops' own time  26.2 us (14%)
  waiting for transfers between devices  25.1 us (13%)
  blocking collectives  20.3 us (11%)
  matrix products  14.5 us (8%)
  between operations  13.6 us (7%)
    all_gather x1, waiting for transfers between devices, attend(): kv_piece = lax.all_gather(packed_pair, 'srv', axis=0, tiled=True)  25.1 us
    another operation x1, loops' own time, attend(): lax.scan(one_step, running, (shards, jnp.arange(shard_count, dtype=jnp.in...  24.9 us
    all_to_all x1, blocking collectives, trade_parts(): received = lax.all_to_all(jnp.stack(pieces), mesh_axis, 0, 0)  20.3 us
    slice x8, local copies, waits for them, and re-layouts, add_shard(): state[2][row_slice]  14.1 us
    dynamic_slice x24, local copies, waits for them, and re-layouts, attend(): lax.scan(one_step, running, (shards, jnp.arange(shard_count, dtype=jnp.in...  13.5 us
    concatenate x8, other arithmetic, add_shard(): jnp.concatenate([item[2] for item in updated], axis=0)  11.9 us
    add x20, other arithmetic, merge_shard(): run_acc * old_factor[..., None] + part_value * new_factor[..., None]  10.1 us
    reduce_sum x20, other arithmetic, merge_shard(): shard_total = jnp.sum(weights, axis=3)  8.24 us
  transfers between devices with their start and end apart: 1, of which 1 were waited for; matrix products, arithmetic and copies ran while one was open for 2% of the time, Pallas kernels for 0%

profile of v1, /device:TPU:6, one launch (start us, length us, event | category | flops | bytes accessed | tf_op | source)
XLA Modules:
  0.0 185.6 jit_solution(15930331983388430414)
XLA Ops:
  13.4 25.1 %all-gather.2.cloned.1.call-done = bf16[2048,512]{0,1:T(8,128)(2,1)} async-done(((bf16[256,512]{0,1:T(8,128)(2,1)}), bf16[2048,512]{0,1:T(8,128)(2,1)}) %all-gather.2.cloned.1.call-update) | async-done | bytes 2097168 | tf_op jit(solution)/shard_map/all_gather | solution.py:113
  38.4 3.9 %copy.52 = bf16[2048,512]{1,0:T(8,128)(2,1)} copy(bf16[2048,512]{0,1:T(8,128)(2,1)} %all-gather.2.cloned.1.call-done) | data formatting | bytes 4194304 | tf_op jit(solution)/shard_map/all_gather | solution.py:113
  43.9 110.0 %while.18 = (s32[]{:T(128)}, f32[256,16]{0,1:T(8,128)S(1)}, f32[256,16]{0,1:T(8,128)S(1)}, f32[256,16,128]{2,0,1:T(8,128)}, s32[256]{0:T(256)S(1)}, /*index=5*/s...) while((s32[]{:T(128)}, f32[256,16]{0,1:T(8,128)S(1)}, ...), condition=%wide.region_23.24_spmd, body=%wide.region_2.23_spmd.sunk | while | flops 549692672 | bytes 33666752 | solution.py:121
  46.4 1.8 fusion.82
  55.4 1.8 fusion.82
  64.5 1.8 fusion.82
  67.7 1.8 conditional.11
  70.0 1.9 %conditional.10 = ((f32[64,16]{0,1:T(8,128)S(1)}, f32[64,16]{0,1:T(8,128)S(1)}, f32[64,16,128]{2,0,1:T(8,128)S(1)})) conditional(s32[]{:T(128)} %convert_element_type.107, (f32[64,16]{0,1:T(8,128)S(1)}, f32[64,16]{0,1:T(8,128)S(1)}, f32[64,16,128]{2,0,1:T(8,128)S(1)}) %tuple.137, (s32[256]{0:T(256)S(1)}, s32[256]{0:T(256)S(1)}, s32[256]{0:T(256)S(1)}, ...), branch_computations={%region_9.9_spmd, %region_10.12_spmd} | conditional | flops 137023488 | bytes 5892640 | solution.py:86
  72.6 1.8 conditional.9
  75.0 1.9 %conditional.8 = ((f32[64,16]{0,1:T(8,128)S(1)}, f32[64,16]{0,1:T(8,128)S(1)}, f32[64,16,128]{2,0,1:T(8,128)S(1)})) conditional(s32[]{:T(128)} %convert_element_type.105, (f32[64,16]{0,1:T(8,128)S(1)}, f32[64,16]{0,1:T(8,128)S(1)}, f32[64,16,128]{2,0,1:T(8,128)S(1)}) %tuple.133, (s32[256]{0:T(256)S(1)}, s32[256]{0:T(256)S(1)}, s32[256]{0:T(256)S(1)}, ...), branch_computations={%region_19.19_spmd, %region_20.22_spmd} | conditional | flops 137023488 | bytes 5892640 | solution.py:86
  81.1 1.8 fusion.82
  84.2 1.8 conditional.11
  86.6 1.9 %conditional.10 = ((f32[64,16]{0,1:T(8,128)S(1)}, f32[64,16]{0,1:T(8,128)S(1)}, f32[64,16,128]{2,0,1:T(8,128)S(1)})) conditional(s32[]{:T(128)} %convert_element_type.107, (f32[64,16]{0,1:T(8,128)S(1)}, f32[64,16]{0,1:T(8,128)S(1)}, f32[64,16,128]{2,0,1:T(8,128)S(1)}) %tuple.137, (s32[256]{0:T(256)S(1)}, s32[256]{0:T(256)S(1)}, s32[256]{0:T(256)S(1)}, ...), branch_computations={%region_9.9_spmd, %region_10.12_spmd} | conditional | flops 137023488 | bytes 5892640 | solution.py:86
  89.2 1.8 conditional.9
  91.6 1.9 %conditional.8 = ((f32[64,16]{0,1:T(8,128)S(1)}, f32[64,16]{0,1:T(8,128)S(1)}, f32[64,16,128]{2,0,1:T(8,128)S(1)})) conditional(s32[]{:T(128)} %convert_element_type.105, (f32[64,16]{0,1:T(8,128)S(1)}, f32[64,16]{0,1:T(8,128)S(1)}, f32[64,16,128]{2,0,1:T(8,128)S(1)}) %tuple.133, (s32[256]{0:T(256)S(1)}, s32[256]{0:T(256)S(1)}, s32[256]{0:T(256)S(1)}, ...), branch_computations={%region_19.19_spmd, %region_20.22_spmd} | conditional | flops 137023488 | bytes 5892640 | solution.py:86
  100.8 1.8 conditional.11
  103.1 1.9 %conditional.10 = ((f32[64,16]{0,1:T(8,128)S(1)}, f32[64,16]{0,1:T(8,128)S(1)}, f32[64,16,128]{2,0,1:T(8,128)S(1)})) conditional(s32[]{:T(128)} %convert_element_type.107, (f32[64,16]{0,1:T(8,128)S(1)}, f32[64,16]{0,1:T(8,128)S(1)}, f32[64,16,128]{2,0,1:T(8,128)S(1)}) %tuple.137, (s32[256]{0:T(256)S(1)}, s32[256]{0:T(256)S(1)}, s32[256]{0:T(256)S(1)}, ...), branch_computations={%region_9.9_spmd, %region_10.12_spmd} | conditional | flops 137023488 | bytes 5892640 | solution.py:86
  105.7 1.8 conditional.9
  108.1 1.9 %conditional.8 = ((f32[64,16]{0,1:T(8,128)S(1)}, f32[64,16]{0,1:T(8,128)S(1)}, f32[64,16,128]{2,0,1:T(8,128)S(1)})) conditional(s32[]{:T(128)} %convert_element_type.105, (f32[64,16]{0,1:T(8,128)S(1)}, f32[64,16]{0,1:T(8,128)S(1)}, f32[64,16,128]{2,0,1:T(8,128)S(1)}) %tuple.133, (s32[256]{0:T(256)S(1)}, s32[256]{0:T(256)S(1)}, s32[256]{0:T(256)S(1)}, ...), branch_computations={%region_19.19_spmd, %region_20.22_spmd} | conditional | flops 137023488 | bytes 5892640 | solution.py:86
  114.2 1.8 fusion.82
  117.3 1.8 conditional.11
  119.7 1.9 %conditional.10 = ((f32[64,16]{0,1:T(8,128)S(1)}, f32[64,16]{0,1:T(8,128)S(1)}, f32[64,16,128]{2,0,1:T(8,128)S(1)})) conditional(s32[]{:T(128)} %convert_element_type.107, (f32[64,16]{0,1:T(8,128)S(1)}, f32[64,16]{0,1:T(8,128)S(1)}, f32[64,16,128]{2,0,1:T(8,128)S(1)}) %tuple.137, (s32[256]{0:T(256)S(1)}, s32[256]{0:T(256)S(1)}, s32[256]{0:T(256)S(1)}, ...), branch_computations={%region_9.9_spmd, %region_10.12_spmd} | conditional | flops 137023488 | bytes 5892640 | solution.py:86
  122.3 1.8 conditional.9
  124.7 1.9 %conditional.8 = ((f32[64,16]{0,1:T(8,128)S(1)}, f32[64,16]{0,1:T(8,128)S(1)}, f32[64,16,128]{2,0,1:T(8,128)S(1)})) conditional(s32[]{:T(128)} %convert_element_type.105, (f32[64,16]{0,1:T(8,128)S(1)}, f32[64,16]{0,1:T(8,128)S(1)}, f32[64,16,128]{2,0,1:T(8,128)S(1)}) %tuple.133, (s32[256]{0:T(256)S(1)}, s32[256]{0:T(256)S(1)}, s32[256]{0:T(256)S(1)}, ...), branch_computations={%region_19.19_spmd, %region_20.22_spmd} | conditional | flops 137023488 | bytes 5892640 | solution.py:86
  130.8 1.8 fusion.82
  133.9 1.8 conditional.11
  136.3 1.9 %conditional.10 = ((f32[64,16]{0,1:T(8,128)S(1)}, f32[64,16]{0,1:T(8,128)S(1)}, f32[64,16,128]{2,0,1:T(8,128)S(1)})) conditional(s32[]{:T(128)} %convert_element_type.107, (f32[64,16]{0,1:T(8,128)S(1)}, f32[64,16]{0,1:T(8,128)S(1)}, f32[64,16,128]{2,0,1:T(8,128)S(1)}) %tuple.137, (s32[256]{0:T(256)S(1)}, s32[256]{0:T(256)S(1)}, s32[256]{0:T(256)S(1)}, ...), branch_computations={%region_9.9_spmd, %region_10.12_spmd} | conditional | flops 137023488 | bytes 5892640 | solution.py:86
  138.8 1.8 conditional.9
  141.3 1.9 %conditional.8 = ((f32[64,16]{0,1:T(8,128)S(1)}, f32[64,16]{0,1:T(8,128)S(1)}, f32[64,16,128]{2,0,1:T(8,128)S(1)})) conditional(s32[]{:T(128)} %convert_element_type.105, (f32[64,16]{0,1:T(8,128)S(1)}, f32[64,16]{0,1:T(8,128)S(1)}, f32[64,16,128]{2,0,1:T(8,128)S(1)}) %tuple.133, (s32[256]{0:T(256)S(1)}, s32[256]{0:T(256)S(1)}, s32[256]{0:T(256)S(1)}, ...), branch_computations={%region_19.19_spmd, %region_20.22_spmd} | conditional | flops 137023488 | bytes 5892640 | solution.py:86
  147.3 1.8 fusion.82
  153.9 1.9 %divide_convert_fusion = bf16[256,16,128]{2,0,1:T(8,128)(2,1)S(1)} fusion(f32[256,16,128]{2,0,1:T(8,128)} %get-tuple-element.329, f32[256,16]{0,1:T(8,128)S(1)} %get-tuple-element.330), kind=kLoop, calls=%fused_computation.104 | loop fusion | flops 1048576 | bytes 3162112 | tf_op jit(solution)/shard_map/convert_element_type | solution.py:123
  157.3 20.3 %all_to_all.5 = bf16[4,64,2048]{2,1,0:T(8,128)(2,1)S(1)} all-to-all(bf16[4,64,2048]{2,1,0:T(8,128)(2,1)S(1)} %pad_maximum_fusion.4), channel_id=1, replica_groups=mesh['srv'=8,'head'=4] {'head'}, dimensions={0} | all-to-all | bytes 2097152 | tf_op jit(solution)/shard_map/all_to_all | solution.py:12
  (290 shorter events, 82.3 us)
Async XLA Ops:
  6.5 3.6 %copy-start = (bf16[256,2048]{1,0:T(8,128)(2,1)S(1)}, bf16[256,2048]{1,0:T(8,128)(2,1)}, u32[]{:S(2)}) copy-start(bf16[256,2048]{1,0:T(8,128)(2,1)} %param.13) | copy-start | bytes 3145732
  6.5 31.9 %all-gather.2.cloned.1.call-start = ((), (), s32[]{:S(2)}) async-start(), calls=%async_computation.1 | async-start | bytes 2359296 | tf_op jit(solution)/shard_map/all_gather | solution.py:113
Sparse Core Ops, SparseCore 0:
  10.0 28.3 all-gather.1
